TPU v7x, 512 devices: a whole 4x4x16 slice. The times are simulated.
512 devices in a mesh: head: 8 (over x, core), ctx: 64 (over y, z).
Axes of the slice: x: 4, y: 4, z: 16, core: 2. Of those that a mesh axis runs over, the one named last changes fastest.
Arguments:
- queries: bfloat16 [8, 64, 1024, 128], P('head', 'ctx'), may hold values from -72 to 72
- keys: bfloat16 [8, 262144, 128], P('head', 'ctx'), may hold values from -24 to 24
- values: bfloat16 [8, 262144, 128], P('head', 'ctx'), may hold values from -6 to 6
- kept: int32 [8, 512], P('head'), may hold values from 0 to 262143, as said below
- roots: int32 [8], P('head'), may hold values from 0 to 63
Outputs:
- compact: float32 [8, 512, 128], P('head')
- fit_error: float32 [], replicated
Inputs may be any that keep to these rules, and one draw needn't show every extreme that they name: `kept`: per head: 512 distinct increasing positions; at most 32 of them lie within one context device's 4096 positions, and exactly 32 within at least one such device.
All inputs are finite; a program needn't handle non-finite values.
Results may differ from a plain program's by a relative error of at most 0.0003.
Values may be sent and summed in bfloat16 or wider, within the bound.
A program may use at most 64 MiB of HBM per device.

v0:
```python
import math
import jax
import jax.numpy as jnp
from jax import lax
from jax.sharding import PartitionSpec as P

HD = 128
KBLK = 1024
M = 512
ridge_share = 0.01


def spread(array, axis, root):
    mine = lax.axis_index(axis) == root
    return lax.psum(jnp.where(mine, array, jnp.zeros_like(array)), axis)


def merge_parts(first, second):
    first_max, first_sum, first_out = first
    second_max, second_sum, second_out = second
    joint = jnp.maximum(first_max, second_max)
    first_scale = jnp.exp(first_max - joint)
    second_scale = jnp.exp(second_max - joint)
    return (
        joint,
        first_sum * first_scale + second_sum * second_scale,
        first_out * first_scale[:, None] + second_out * second_scale[:, None],
    )


def block_partials(queries_ref, key_slab, value_slab, score_scale):
    blocks = key_slab.shape[0] // KBLK
    key_blocks = key_slab.reshape(blocks, KBLK, HD)
    value_blocks = value_slab.reshape(blocks, KBLK, HD)
    rows = queries_ref.shape[0]

    def visit(carry, pieces):
        key_block, value_block = pieces
        scores = (
            jnp.einsum("rd,kd->rk", queries_ref, key_block, preferred_element_type=jnp.float32)
            * score_scale
        )
        block_max = jnp.max(scores, axis=1)
        weights = jnp.exp(scores - block_max[:, None]).astype(jnp.bfloat16)
        block_sum = jnp.sum(weights.astype(jnp.float32), axis=1)
        block_out = jnp.dot(weights, value_block, preferred_element_type=jnp.float32)
        return (merge_parts(carry, (block_max, block_sum, block_out)), None)

    start = (
        jnp.full((rows,), -jnp.inf, jnp.float32),
        jnp.zeros((rows,), jnp.float32),
        jnp.zeros((rows, HD), jnp.float32),
    )
    return lax.scan(visit, start, (key_blocks, value_blocks))[0]


def compact_softmax(queries_ref, compact_keys, score_scale):
    scores = (
        jnp.einsum("rd,md->rm", queries_ref, compact_keys, preferred_element_type=jnp.float32)
        * score_scale
    )
    return jax.nn.softmax(scores, axis=1)


def inner_left(left, right):
    return lax.dot_general(
        left,
        right,
        (((0,), (0,)), ((), ())),
        precision=lax.Precision.HIGHEST,
        preferred_element_type=jnp.float32,
    )


def per_device(queries, keys, values, kept, roots):
    score_scale = 1.0 / math.sqrt(HD)
    queries_ref = spread(queries[0, 0], "ctx", roots[0])
    run_max, run_sum, run_out = block_partials(queries_ref, keys[0], values[0], score_scale)
    highest = lax.pmax(run_max, "ctx")
    rescale = jnp.exp(run_max - highest)
    run_sum, run_out = lax.psum((run_sum * rescale, run_out * rescale[:, None]), "ctx")
    target = run_out / run_sum[:, None]
    slab = keys.shape[1]
    shard = lax.axis_index("ctx")
    positions = kept[0]
    owner = positions // slab
    local_rows = positions - shard * slab
    mine = owner == shard
    picked = jnp.take(keys[0], jnp.clip(local_rows, 0, slab - 1), axis=0).astype(jnp.float32)
    picked = picked * mine.astype(jnp.float32)[:, None]
    compact_keys = lax.psum(picked, "ctx").astype(jnp.bfloat16)
    attend = compact_softmax(queries_ref, compact_keys, score_scale)
    gram = inner_left(attend, attend)
    cross = inner_left(attend, target)
    ridge = ridge_share * jnp.trace(gram) / M
    system = gram + ridge * jnp.eye(M, dtype=jnp.float32)
    factor_low = jnp.linalg.cholesky(system)
    halfway = lax.linalg.triangular_solve(factor_low, cross, left_side=True, lower=True)
    compact = lax.linalg.triangular_solve(
        factor_low, halfway, left_side=True, lower=True, transpose_a=True
    )
    target_square = jnp.sum(target * target)
    fitted_square = jnp.sum(
        compact
        * jnp.dot(
            gram, compact, precision=lax.Precision.HIGHEST, preferred_element_type=jnp.float32
        )
    )
    head_error = (target_square - 2.0 * jnp.sum(compact * cross) + fitted_square) / target_square
    fit_error = lax.psum(head_error, "head") / lax.axis_size("head")
    return (compact[None], fit_error)


def solution(mesh):
    placed = (
        P("head", "ctx", None, None),
        P("head", "ctx", None),
        P("head", "ctx", None),
        P("head", None),
        P("head"),
    )
    return jax.shard_map(
        per_device,
        mesh=mesh,
        in_specs=placed,
        out_specs=(P("head", None, None), P()),
        check_vma=False,
    )
```

profile of v0, /device:TPU:1, one launch (start us, length us, event | category | flops | bytes accessed | tf_op | source)
XLA Modules:
  0.0 929.7 jit_solution(15579256206267281522)
XLA Ops:
  7.9 0.7 select_bitcast_fusion
  8.7 0.7 compare_select_fusion
  9.4 0.7 compare_and_fusion
  10.1 2.4 gather_fusion
  12.7 260.3 %all-reduce.6.cloned.1.call-done = bf16[1024,128]{1,0:T(8,128)(2,1)} async-done(((bf16[1024,128]{1,0:T(8,128)(2,1)}), bf16[1024,128]{1,0:T(8,128)(2,1)}) %all-reduce.6.cloned.1.call-update) | async-done | bytes 262160 | tf_op jit(solution)/shard_map/psum | solution.py:15
  273.0 31.4 %while.17 = (s32[]{:T(128)}, f32[1024]{0:T(1024)S(1)}, f32[1024]{0:T(1024)S(1)}, f32[1024,128]{1,0:T(8,128)S(1)}, bf16[4,1024,128]{2,1,0:T(8,128)(2,1)}, /*index...) while((s32[]{:T(128)}, f32[1024]{0:T(1024)S(1)}, ...), condition=%wide.region_16.17_spmd.clone, body=%wide.region_13.16_spmd.clone.sunk | while | flops 547887104 | bytes 31252628 | solution.py:54
  273.0 1.7 multiply_reduce_fusion.5
  274.8 1.9 copy-done
  276.7 0.7 convert_reduce_fusion.2
  277.4 3.4 fusion.100
  280.8 1.7 multiply_reduce_fusion.5
  282.6 1.9 copy-done
  284.5 0.7 convert_reduce_fusion.2
  285.3 3.4 fusion.100
  288.7 1.7 multiply_reduce_fusion.5
  290.5 1.9 copy-done
  292.4 0.7 convert_reduce_fusion.2
  293.1 3.4 fusion.100
  296.5 1.7 multiply_reduce_fusion.5
  298.3 1.9 copy-done
  300.2 0.7 convert_reduce_fusion.2
  301.0 3.4 fusion.100
  304.4 113.1 %pmax.7 = f32[1024]{0:T(1024)S(1)} all-reduce(f32[1024]{0:T(1024)S(1)} %get-tuple-element.42), channel_id=1, replica_groups=mesh['head'=8,'ctx'=64] {'ctx'}, use_global_device_ids=true, to_apply=%region_17.18 | all-reduce | flops 1024 | bytes 8192 | tf_op jit(solution)/shard_map/pmax | solution.py:79
  417.5 1.0 broadcast_multiply_fusion
  418.5 222.3 %all-reduce.9 = (bf16[512,128]{1,0:T(8,128)(2,1)S(1)}, f32[1024]{0:T(1024)S(1)}) all-reduce(f32[512,128]{1,0:T(8,128)S(1)} %convert_multiply_fusion, f32[1024]{0:T(1024)S(1)} %get-tuple-element.104), channel_id=1, replica_groups=mesh['head'=8,'ctx'=64] {'ctx'}, use_global_device_ids=true, to_apply=%region_1.2 | all-reduce | flops 66560 | bytes 401408 | tf_op jit(solution)/shard_map/psum | solution.py:91
  640.8 1.4 multiply_reduce_fusion.1
  642.6 4.7 select_reduce_fusion
  647.3 1.3 copy.8
  649.3 1.4 fusion.13
  650.8 1.0 copy-done.2
  651.8 11.7 %cholesky.103 = f32[128,128]{1,0:T(8,128)S(1)} custom-call(f32[128,128]{1,0:T(8,128)S(1)} %cholesky.263), custom_call_target="Cholesky" | custom-call | tf_op jit(solution)/shard_map/jit(cholesky)/cholesky | solution.py:97
  663.5 1.2 cholesky.222
  664.7 9.8 %custom-call.32 = f32[1,128,128]{1,2,0:T(8,128)S(1)} custom-call(f32[1,128,128]{2,1,0:T(8,128)S(1)} %get-tuple-element.121), custom_call_target="InvertDiagBlocksLowerTriangular" | custom-call | tf_op jit(solution)/shard_map/jit(cholesky)/cholesky | solution.py:97
  674.5 2.0 constant_dynamic-update-slice_fusion.3
  676.4 1.2 convolution_subtract_fusion
  677.7 12.2 %cholesky.215 = f32[128,128]{1,0:T(8,128)S(1)} custom-call(f32[128,128]{1,0:T(8,128)S(1)} %cholesky.267), custom_call_target="Cholesky" | custom-call | tf_op jit(solution)/shard_map/jit(cholesky)/cholesky | solution.py:97
  689.9 0.6 select_reduce_fusion.3
  690.6 9.8 %custom-call.33 = f32[1,128,128]{1,2,0:T(8,128)S(1)} custom-call(f32[1,128,128]{2,1,0:T(8,128)S(1)} %get-tuple-element.118), custom_call_target="InvertDiagBlocksLowerTriangular" | custom-call | tf_op jit(solution)/shard_map/jit(cholesky)/cholesky | solution.py:97
  700.4 0.9 convolution_dynamic-update-slice_fusion
  701.3 1.4 convolution_subtract_fusion.1
  702.8 11.7 %cholesky.236 = f32[128,128]{1,0:T(8,128)S(1)} custom-call(f32[128,128]{1,0:T(8,128)S(1)} %cholesky.272), custom_call_target="Cholesky" | custom-call | tf_op jit(solution)/shard_map/jit(cholesky)/cholesky | solution.py:97
  714.5 0.6 select_reduce_fusion.2
  715.1 9.8 %custom-call.34 = f32[1,128,128]{1,2,0:T(8,128)S(1)} custom-call(f32[1,128,128]{2,1,0:T(8,128)S(1)} %get-tuple-element.115), custom_call_target="InvertDiagBlocksLowerTriangular" | custom-call | tf_op jit(solution)/shard_map/jit(cholesky)/cholesky | solution.py:97
  724.9 0.8 convolution_dynamic-update-slice_fusion.1
  725.8 1.6 convolution_subtract_fusion.8
  727.4 11.7 %cholesky.253 = f32[128,128]{1,0:T(8,128)S(1)} custom-call(f32[128,128]{1,0:T(8,128)S(1)} %convolution_subtract_fusion.8), custom_call_target="Cholesky" | custom-call | tf_op jit(solution)/shard_map/jit(cholesky)/cholesky | solution.py:97
  739.1 0.7 select_reduce_fusion.1
  739.7 0.7 compare_reduce_fusion.1
  740.4 0.6 compare_reduce_fusion
  741.1 0.7 compare_reduce_fusion.2
  744.3 2.4 select_select_fusion
  746.6 14.4 %while.16 = (s32[]{:T(128)}, f32[512,512]{1,0:T(8,128)}, s32[4,2]{0,1:T(2,128)S(1)}, f32[4,128,128]{2,1,0:T(8,128)}, s32[]{:T(128)}) while((s32[]{:T(128)}, f32[512,512]{1,0:T(8,128)}, s32[4,2]{0,1:T(2,128)S(1)}, f32[4,128,128]{2,1,0:T(8,128)}, s32[]{:T(128)}) %tuple.64), condition=%wide.while_cond, body=%wide.while_body.sunk | while | flops 2 | bytes 132205 | solution.py:99
  746.7 0.6 fusion.96
  747.3 3.0 bitcast_dynamic-update-slice_fusion.2
  750.3 0.6 fusion.96
  750.9 3.0 bitcast_dynamic-update-slice_fusion.2
  754.6 3.0 bitcast_dynamic-update-slice_fusion.2
  758.2 2.9 bitcast_dynamic-update-slice_fusion.2
  761.1 40.3 %custom-call.35 = f32[4,128,128]{1,2,0:T(8,128)S(1)} custom-call(f32[4,128,128]{2,1,0:T(8,128)} %get-tuple-element.51), custom_call_target="InvertDiagBlocksLowerTriangular" | custom-call | tf_op jit(solution)/shard_map/triangular_solve | solution.py:99
  801.4 3.2 fusion.15
  808.7 1.3 multiply_reduce_fusion.3
  810.0 1.7 fusion.14
  812.3 0.8 multiply_reduce_fusion.2
  815.1 105.7 %psum.39 = f32[]{:T(128)} all-reduce(f32[]{:T(128)S(6)} %div.56), channel_id=1, replica_groups=mesh['head'=8,'ctx'=64] {'head'}, use_global_device_ids=true, to_apply=%region_23.24 | all-reduce | flops 1 | bytes 8 | tf_op jit(solution)/shard_map/psum | solution.py:110
  (52 shorter events, 6.2 us)
Async XLA Ops:
  7.2 265.8 %all-reduce.6.cloned.1.call-start = ((), (), s32[]{:S(2)}) async-start(), calls=%async_computation | async-start | bytes 524288 | tf_op jit(solution)/shard_map/psum | solution.py:15
  8.6 792.8 %all-reduce.8.cloned.1.call-start = ((), (), s32[]{:S(2)}) async-start(), calls=%async_computation.1 | async-start | bytes 1048576 | tf_op jit(solution)/shard_map/psum | solution.py:81
  274.7 1.9 copy-start
  282.6 1.9 copy-start
  290.4 1.9 copy-start
  298.3 1.9 copy-start
  650.7 1.0 copy-start.2
  801.4 3.5 copy-start.1
  806.3 6.0 copy-start.3
Sparse Core Ops, SparseCore 0:
  12.0 260.9 all-reduce.5
  418.6 285.3 all-reduce.7
where the time goes:
time: 934 us; the launch traced here: 930 us
  blocking collectives  441 us (47%)
  waiting for transfers between devices  260 us (28%)
  other arithmetic  134 us (14%)
  matrix products  43.4 us (5%)
  local copies, waits for them, and re-layouts  28 us (3%)
  between operations  22.9 us (2%)
    psum x1, waiting for transfers between devices, spread(): return lax.psum(jnp.where(mine, array, jnp.zeros_like(array)), axis)  260 us
    psum x1, blocking collectives, per_device(): compact_keys = lax.psum(picked, 'ctx').astype(jnp.bfloat16)  222 us
    pmax x1, blocking collectives, per_device(): highest = lax.pmax(run_max, 'ctx')  113 us
    psum x1, blocking collectives, per_device(): fit_error = lax.psum(head_error, 'head') / lax.axis_size('head')  106 us
    another operation x14, other arithmetic, per_device(): factor_low = jnp.linalg.cholesky(system)  80.8 us
    another operation x3, other arithmetic, per_device(): lax.linalg.triangular_solve(factor_low, halfway, left_side=True, lower=Tr...  42.7 us
  transfers between devices with their start and end apart: 2, of which 1 were waited for; matrix products, arithmetic and copies ran while one was open for 17% of the time, Pallas kernels for 0%

commit v1 on v0

--- a/solution.py
+++ b/solution.py
@@ -12,7 +12,7 @@
 
 def spread(array, axis, root):
     mine = lax.axis_index(axis) == root
-    return lax.psum(jnp.where(mine, array, jnp.zeros_like(array)), axis)
+    return jnp.sum(lax.all_gather(jnp.where(mine, array, jnp.zeros_like(array)), axis), axis=0)
 
 
 def merge_parts(first, second):

time: 934 us -> 1060 us (1.13)
  waiting for transfers between devices: 260 us -> 473 us
  blocking collectives: 441 us -> 358 us
    psum x1, waiting for transfers between devices: 0.02 us -> 277 us  [per_device(): lax.psum((run_sum * rescale, run_out * rescale[:, None]), 'ctx')]
    psum x1 -> x0, waiting for transfers between devices: 260 us -> none  [spread(): return lax.psum(jnp.where(mine, array, jnp.zeros_like(array)), axis)]
    all_gather x0 -> x1, waiting for transfers between devices: none -> 196 us  [spread(): lax.all_gather(jnp.where(mine, array, jnp.zeros_like(array)), axis)]
    psum x1, blocking collectives: 106 us -> 23 us  [per_device(): fit_error = lax.psum(head_error, 'head') / lax.axis_size('head')]
  transfers between devices with their start and end apart: 2 -> 2, of which waited for: 1 -> 2; matrix products, arithmetic and copies ran while one was open for 17% -> 5% of each run, Pallas kernels for 0% -> 0%
where the time goes in v1:
time: 1060 us; the launch traced here: 1050 us
  waiting for transfers between devices  473 us (45%)
  blocking collectives  358 us (34%)
  other arithmetic  137 us (13%)
  matrix products  40.5 us (4%)
  local copies, waits for them, and re-layouts  22.9 us (2%)
  between operations  22.9 us (2%)
    psum x1, waiting for transfers between devices, per_device(): lax.psum((run_sum * rescale, run_out * rescale[:, None]), 'ctx')  277 us
    psum x1, blocking collectives, per_device(): compact_keys = lax.psum(picked, 'ctx').astype(jnp.bfloat16)  223 us
    all_gather x1, waiting for transfers between devices, spread(): lax.all_gather(jnp.where(mine, array, jnp.zeros_like(array)), axis)  196 us
    pmax x1, blocking collectives, per_device(): highest = lax.pmax(run_max, 'ctx')  112 us
    another operation x14, other arithmetic, per_device(): factor_low = jnp.linalg.cholesky(system)  78.9 us
    another operation x3, other arithmetic, per_device(): lax.linalg.triangular_solve(factor_low, halfway, left_side=True, lower=Tr...  40.6 us
    psum x1, blocking collectives, per_device(): fit_error = lax.psum(head_error, 'head') / lax.axis_size('head')  23 us
  transfers between devices with their start and end apart: 2, of which 2 were waited for; matrix products, arithmetic and copies ran while one was open for 5% of the time, Pallas kernels for 0%

profile of v1, /device:TPU:1, one launch (start us, length us, event | category | flops | bytes accessed | tf_op | source)
XLA Modules:
  0.0 1054.9 jit_solution(16757393772805951007)
XLA Ops:
  7.9 0.7 broadcast_select_fusion
  8.7 0.7 compare_select_fusion
  9.4 2.4 gather_fusion
  11.8 0.7 compare_and_fusion
  12.7 196.2 %all-gather.3.cloned.1.call-done = bf16[64,1,1024,128]{3,2,1,0:T(8,128)(2,1)} async-done(((bf16[1,1,1024,128]{3,2,1,0:T(8,128)(2,1)}), bf16[64,1,1024,128]{3,2,1,0:T(8,128)(2,1)}) %all-gather.3.cloned.1.call-update) | async-done | bytes 16777232 | tf_op jit(solution)/shard_map/all_gather | solution.py:15
  209.0 8.8 reduce_sum.67
  217.8 31.1 %while.17 = (s32[]{:T(128)}, f32[1024]{0:T(1024)S(1)}, f32[1024]{0:T(1024)S(1)}, f32[1024,128]{1,0:T(8,128)S(1)}, bf16[4,1024,128]{2,1,0:T(8,128)(2,1)}, /*index...) while((s32[]{:T(128)}, f32[1024]{0:T(1024)S(1)}, ...), condition=%wide.region_16.17_spmd.clone, body=%wide.region_13.16_spmd.clone.sunk | while | flops 547887104 | bytes 31253636 | solution.py:54
  217.8 1.7 multiply_reduce_fusion.5
  219.5 1.9 copy-done
  221.4 0.7 convert_reduce_fusion.2
  222.1 3.4 fusion.100
  225.5 1.7 multiply_reduce_fusion.5
  227.2 1.9 copy-done
  229.1 0.7 convert_reduce_fusion.2
  229.9 3.4 fusion.100
  233.3 1.7 multiply_reduce_fusion.5
  235.0 1.9 copy-done
  236.9 0.7 convert_reduce_fusion.2
  237.7 3.4 fusion.100
  241.1 1.7 multiply_reduce_fusion.5
  242.8 1.9 copy-done
  244.7 0.7 convert_reduce_fusion.2
  245.4 3.4 fusion.100
  248.8 111.9 %pmax.7 = f32[1024]{0:T(1024)S(1)} all-reduce(f32[1024]{0:T(1024)S(1)} %get-tuple-element.42), channel_id=1, replica_groups=mesh['head'=8,'ctx'=64] {'ctx'}, use_global_device_ids=true, to_apply=%region_17.18 | all-reduce | flops 1024 | bytes 8192 | tf_op jit(solution)/shard_map/pmax | solution.py:79
  360.7 222.8 %all-reduce.6 = (bf16[512,128]{1,0:T(8,128)(2,1)S(1)}, f32[1024]{0:T(1024)S(1)}) all-reduce(f32[512,128]{1,0:T(8,128)S(1)} %convert_multiply_fusion, f32[1024]{0:T(1024)S(1)} %get-tuple-element.104), channel_id=1, replica_groups=mesh['head'=8,'ctx'=64] {'ctx'}, use_global_device_ids=true, to_apply=%region_1.2 | all-reduce | flops 66560 | bytes 401408 | tf_op jit(solution)/shard_map/psum | solution.py:91
  583.5 0.4 multiply_reduce_fusion.1
  584.0 0.4 fusion.11
  584.3 4.7 select_reduce_fusion
  590.3 1.0 copy-done.3
  591.3 11.7 %cholesky.103 = f32[128,128]{1,0:T(8,128)S(1)} custom-call(f32[128,128]{1,0:T(8,128)S(1)} %cholesky.263), custom_call_target="Cholesky" | custom-call | tf_op jit(solution)/shard_map/jit(cholesky)/cholesky | solution.py:97
  603.2 9.8 custom-call.32
  613.0 1.2 constant_dynamic-update-slice_fusion.3
  614.2 1.3 convolution_subtract_fusion
  615.5 12.2 %cholesky.215 = f32[128,128]{1,0:T(8,128)S(1)} custom-call(f32[128,128]{1,0:T(8,128)S(1)} %cholesky.267), custom_call_target="Cholesky" | custom-call | tf_op jit(solution)/shard_map/jit(cholesky)/cholesky | solution.py:97
  627.8 9.8 custom-call.33
  637.8 1.3 convolution_subtract_fusion.1
  639.1 11.7 %cholesky.236 = f32[128,128]{1,0:T(8,128)S(1)} custom-call(f32[128,128]{1,0:T(8,128)S(1)} %cholesky.272), custom_call_target="Cholesky" | custom-call | tf_op jit(solution)/shard_map/jit(cholesky)/cholesky | solution.py:97
  650.9 0.7 compare_reduce_fusion.1
  651.5 9.8 custom-call.34
  661.4 0.4 convolution_dynamic-update-slice_fusion.1
  661.7 1.2 convolution_subtract_fusion.8
  663.0 11.7 %cholesky.253 = f32[128,128]{1,0:T(8,128)S(1)} custom-call(f32[128,128]{1,0:T(8,128)S(1)} %convolution_subtract_fusion.8), custom_call_target="Cholesky" | custom-call | tf_op jit(solution)/shard_map/jit(cholesky)/cholesky | solution.py:97
  674.7 0.7 compare_reduce_fusion
  675.4 1.0 broadcast_multiply_fusion
  676.4 0.7 compare_reduce_fusion.2
  679.6 1.1 select_select_fusion
  680.7 11.4 %while.16 = (s32[]{:T(128)}, f32[512,512]{1,0:T(8,128)}, s32[4,2]{0,1:T(2,128)S(1)}, f32[4,128,128]{2,1,0:T(8,128)S(1)}, s32[]{:T(128)}) while((s32[]{:T(128)}, f32[512,512]{1,0:T(8,128)}, s32[4,2]{0,1:T(2,128)S(1)}, f32[4,128,128]{2,1,0:T(8,128)S(1)}, s32[]{:T(128)}) %tuple.64), condition=%wide.while_cond, body=%wide.while_body.sunk | while | flops 2 | bytes 131181 | solution.py:99
  680.8 0.5 fusion.96
  681.3 2.3 bitcast_dynamic-update-slice_fusion.2
  683.6 0.5 fusion.96
  684.2 2.3 bitcast_dynamic-update-slice_fusion.2
  686.5 0.5 fusion.96
  687.0 2.3 bitcast_dynamic-update-slice_fusion.2
  689.4 0.5 fusion.96
  689.9 2.2 bitcast_dynamic-update-slice_fusion.2
  692.1 39.5 %custom-call.35 = f32[4,128,128]{1,2,0:T(8,128)S(1)} custom-call(f32[4,128,128]{2,1,0:T(8,128)S(1)} %get-tuple-element.51), custom_call_target="InvertDiagBlocksLowerTriangular" | custom-call | tf_op jit(solution)/shard_map/triangular_solve | solution.py:99
  731.7 277.1 %all-reduce.5.cloned.1.call-done = f32[1024,128]{1,0:T(8,128)} async-done(((f32[1024,128]{1,0:T(8,128)}), f32[1024,128]{1,0:T(8,128)}) %all-reduce.5.cloned.1.call-update) | async-done | bytes 524304 | tf_op jit(solution)/shard_map/psum | solution.py:81
  1008.8 3.8 fusion.15
  1015.3 0.4 convolution_subtract_fusion.2
  1015.9 0.5 convolution_subtract_fusion.6
  1016.6 1.7 fusion.14
  1018.3 1.3 multiply_reduce_fusion.3
  1020.3 0.8 multiply_reduce_fusion.2
  1023.1 23.0 %psum.31 = f32[]{:T(128)} all-reduce(f32[]{:T(128)S(6)} %div.56), channel_id=1, replica_groups=mesh['head'=8,'ctx'=64] {'head'}, use_global_device_ids=true, to_apply=%region_23.24 | all-reduce | flops 1 | bytes 8 | tf_op jit(solution)/shard_map/psum | solution.py:110
  (55 shorter events, 4.8 us)
Async XLA Ops:
  7.2 201.8 %all-gather.3.cloned.1.call-start = ((), (), s32[]{:S(2)}) async-start(), calls=%async_computation.1 | async-start | bytes 17039360 | tf_op jit(solution)/shard_map/all_gather | solution.py:15
  8.6 1000.2 %all-reduce.5.cloned.1.call-start = ((), (), s32[]{:S(2)}) async-start(), calls=%async_computation | async-start | bytes 1048576 | tf_op jit(solution)/shard_map/psum | solution.py:81
  219.4 1.9 copy-start
  227.2 1.9 copy-start
  235.0 1.9 copy-start
  242.8 1.9 copy-start
  583.9 5.1 copy-start.1
  590.3 1.0 copy-start.3
  1008.8 4.1 copy-start.2
  1014.3 6.0 copy-start.4
Sparse Core Ops, SparseCore 0:
  11.5 197.4 all-gather.2
  676.5 332.2 all-reduce.4
